TPU v7x, 32 devices: a whole 2x2x4 slice. The times are simulated.
32 devices in a mesh: rep: 2 (over y), shard: 16 (over z, x, core).
Axes of the slice: x: 2, y: 2, z: 4, core: 2. Of those that a mesh axis runs over, the one named last changes fastest.
Arguments:
- images: bfloat16 [32, 14, 14, 512], P(('rep', 'shard')), may hold values from -6 to 6
- cotangent: bfloat16 [32, 14, 14, 512], P(('rep', 'shard')), may hold values from -6 to 6
- regions: int32 [32, 14, 14], P(('rep', 'shard')), may hold values from 0 to 8, as said below
- w_qkv: bfloat16 [2, 512, 1536], P(None, 'shard'), may hold values from -0.25 to 0.25
- w_proj: bfloat16 [2, 512, 512], P(None, 'shard'), may hold values from -0.75 to 0.75
- w_fc1: bfloat16 [2, 512, 2048], P(None, 'shard'), may hold values from -0.25 to 0.25
- w_fc2: bfloat16 [2, 2048, 512], P(None, 'shard'), may hold values from -0.125 to 0.125
- norm_gains: bfloat16 [2, 2, 512], P(None, None, 'shard'), may hold values from 0.5 to 1.5
- norm_shifts: bfloat16 [2, 2, 512], P(None, None, 'shard'), may hold values from -1.1953125 to 1.1953125
- branch_biases: bfloat16 [2, 4, 512], P(None, None, 'shard'), may hold values from -1.1953125 to 1.1953125
- fc1_bias: bfloat16 [2, 2048], P(None, 'shard'), may hold values from -1.1953125 to 1.1953125
- rel_table: bfloat16 [2, 169, 16], replicated, may hold values from -6 to 6
Outputs:
- images_out: bfloat16 [32, 14, 14, 512], P(('rep', 'shard'))
- images_grad: float32 [32, 14, 14, 512], P(('rep', 'shard'))
- grad_w_qkv: float32 [2, 512, 1536], P(None, 'shard')
- grad_w_proj: float32 [2, 512, 512], P(None, 'shard')
- grad_w_fc1: float32 [2, 512, 2048], P(None, 'shard')
- grad_w_fc2: float32 [2, 2048, 512], P(None, 'shard')
- grad_norm_gains: float32 [2, 2, 512], P(None, None, 'shard')
- grad_norm_shifts: float32 [2, 2, 512], P(None, None, 'shard')
- grad_branch_biases: float32 [2, 4, 512], P(None, None, 'shard')
- grad_fc1_bias: float32 [2, 2048], P(None, 'shard')
- grad_rel_table: float32 [2, 169, 16], replicated
Inputs may be any that keep to these rules, and one draw needn't show every extreme that they name: `regions`: in each image the ids are 3 * (row band) + (column band), the rows and the columns each cut into three bands of consecutive positions.
All inputs are finite; a program needn't handle non-finite values.
Results may differ from a plain program's by a relative error of at most 0.023.
Values may be sent and summed in bfloat16 or wider, within the bound.
A program may use at most 128 MiB of HBM per device.

v0:
```python
import jax
import jax.numpy as jnp
from jax import lax
from jax.sharding import PartitionSpec as P

SIDE = 14
WIN = 7
SHIFT = 3
eps = 1e-05
highest = lax.Precision.HIGHEST
inv_root_two = 0.7071067811865476
inv_root_two_pi = 0.3989422804014327


def layer_norm(values, norm_gain, norm_shift):
    row_mean = jnp.mean(values, axis=-1, keepdims=True)
    centred = values - row_mean
    row_var = jnp.mean(centred * centred, axis=-1, keepdims=True)
    return centred * lax.rsqrt(row_var + eps) * norm_gain + norm_shift


def times_transposed(left, right):
    return lax.dot_general(
        left, right, (((1,), (1,)), ((), ())), preferred_element_type=jnp.float32
    )


def transposed_times(left, right):
    return lax.dot_general(
        left, right, (((0,), (0,)), ((), ())), preferred_element_type=jnp.float32
    )


def gelu_slope(pre_act):
    return 0.5 * (1.0 + lax.erf(pre_act * inv_root_two)) + pre_act * inv_root_two_pi * jnp.exp(
        -0.5 * pre_act * pre_act
    )


def to_windows(grid_data):
    image_count = grid_data.shape[0]
    per_side = SIDE // WIN
    trailing = grid_data.shape[3:]
    blocks = grid_data.reshape((image_count, per_side, WIN, per_side, WIN) + trailing)
    blocks = jnp.swapaxes(blocks, 2, 3)
    return blocks.reshape((image_count * per_side * per_side, WIN * WIN) + trailing)


def from_windows(blocks, image_count):
    per_side = SIDE // WIN
    trailing = blocks.shape[2:]
    grid_data = blocks.reshape((image_count, per_side, per_side, WIN, WIN) + trailing)
    grid_data = jnp.swapaxes(grid_data, 2, 3)
    return grid_data.reshape((image_count, SIDE, SIDE) + trailing)


def onehot_table():
    cell_ids = jnp.arange(WIN * WIN)
    cell_row = cell_ids // WIN
    cell_col = cell_ids % WIN
    table_side = 2 * WIN - 1
    rel_index = (cell_row[:, None] - cell_row[None, :] + WIN - 1) * table_side + (
        cell_col[:, None] - cell_col[None, :] + WIN - 1
    )
    rel_index = rel_index.reshape(-1)
    return (rel_index[:, None] == jnp.arange(table_side * table_side)[None, :]).astype(jnp.float32)


def replica_total(stacked):
    return (
        lax.psum(stacked[0].astype(jnp.bfloat16), "rep").astype(jnp.float32),
        lax.psum(stacked[1].astype(jnp.bfloat16), "rep").astype(jnp.float32),
        lax.psum(stacked[2].astype(jnp.bfloat16), "rep").astype(jnp.float32),
        lax.psum(stacked[3].astype(jnp.bfloat16), "rep").astype(jnp.float32),
        lax.psum(stacked[4].astype(jnp.bfloat16), "rep").astype(jnp.float32),
        lax.psum(stacked[5].astype(jnp.bfloat16), "rep").astype(jnp.float32),
        lax.psum(stacked[6].astype(jnp.bfloat16), "rep").astype(jnp.float32),
        lax.psum(stacked[7].astype(jnp.bfloat16), "rep").astype(jnp.float32),
    )


def body(
    images,
    cotangent,
    regions,
    w_qkv,
    w_proj,
    w_fc1,
    w_fc2,
    norm_gains,
    norm_shifts,
    branch_biases,
    fc1_bias,
    rel_table,
):
    layer_count = w_qkv.shape[0]
    image_count = images.shape[0]
    model_width = w_proj.shape[2]
    head_count = rel_table.shape[2]
    head_dim = model_width // head_count
    query_scale = head_dim ** (-0.5)
    column_scale = jnp.concatenate(
        [
            jnp.full((model_width,), query_scale, jnp.float32),
            jnp.ones((2 * model_width,), jnp.float32),
        ]
    )
    onehot = onehot_table()
    region_win = to_windows(regions)
    region_mask = jnp.where(region_win[:, :, None] == region_win[:, None, :], 0.0, -100.0).astype(
        jnp.float32
    )
    window_count = region_win.shape[0]
    tokens = window_count * WIN * WIN

    def score_bias(layer_num):
        table_rows = jnp.dot(onehot, rel_table[layer_num].astype(jnp.float32), precision=highest)
        bias_full = table_rows.T.reshape(head_count, WIN * WIN, WIN * WIN)[None]
        if layer_num % 2 == 1:
            bias_full = bias_full + region_mask[:, None]
        return bias_full

    def heads_of(flat):
        return flat.reshape(window_count, WIN * WIN, head_count, head_dim)

    residual = images.astype(jnp.float32)
    saved_acts = []
    kept_weights = []
    for layer_num in range(layer_count):
        shifted = layer_num % 2 == 1
        attn_w = (
            lax.all_gather(w_qkv[layer_num], "shard", axis=0, tiled=True),
            lax.all_gather(w_proj[layer_num], "shard", axis=0, tiled=True),
            lax.all_gather(norm_gains[layer_num], "shard", axis=1, tiled=True),
            lax.all_gather(norm_shifts[layer_num], "shard", axis=1, tiled=True),
            lax.all_gather(branch_biases[layer_num], "shard", axis=1, tiled=True),
        )
        mlp_w = (
            lax.all_gather(w_fc1[layer_num], "shard", axis=0, tiled=True),
            lax.all_gather(w_fc2[layer_num], "shard", axis=0, tiled=True),
            lax.all_gather(fc1_bias[layer_num], "shard", axis=0, tiled=True),
        )
        kept_weights.append((attn_w, mlp_w))
        wqkv, wproj, gains, shifts, biases = attn_w
        gains = gains.astype(jnp.float32)
        shifts = shifts.astype(jnp.float32)
        biases = biases.astype(jnp.float32)
        normed = layer_norm(residual, gains[0], shifts[0]).astype(jnp.bfloat16)
        if shifted:
            normed = jnp.roll(normed, (-SHIFT, -SHIFT), axis=(1, 2))
        window_rows = to_windows(normed).reshape(tokens, model_width)
        projected = jnp.dot(window_rows, wqkv, preferred_element_type=jnp.float32)
        queries = heads_of(
            ((projected[:, :model_width] + biases[0]) * query_scale).astype(jnp.bfloat16)
        )
        key_rows = heads_of(projected[:, model_width : 2 * model_width].astype(jnp.bfloat16))
        values = heads_of((projected[:, 2 * model_width :] + biases[1]).astype(jnp.bfloat16))
        scores = jnp.einsum(
            "nqhd,nkhd->nhqk", queries, key_rows, preferred_element_type=jnp.float32
        ) + score_bias(layer_num)
        row_max = jnp.max(scores, axis=-1, keepdims=True)
        log_total = row_max + jnp.log(jnp.sum(jnp.exp(scores - row_max), axis=-1, keepdims=True))
        attn_probs = jnp.exp(scores - log_total).astype(jnp.bfloat16)
        mixed_rows = jnp.einsum(
            "nhqk,nkhd->nqhd", attn_probs, values, preferred_element_type=jnp.float32
        )
        mixed_rows = mixed_rows.reshape(tokens, model_width).astype(jnp.bfloat16)
        branch = jnp.dot(mixed_rows, wproj, preferred_element_type=jnp.float32) + biases[2]
        branch = from_windows(branch.reshape(window_count, WIN * WIN, model_width), image_count)
        if shifted:
            branch = jnp.roll(branch, (SHIFT, SHIFT), axis=(1, 2))
        middle = residual + branch
        wfirst, wsecond, bias_first = mlp_w
        normed_mlp = (
            layer_norm(middle, gains[1], shifts[1]).astype(jnp.bfloat16).reshape(-1, model_width)
        )
        pre_act = jnp.dot(
            normed_mlp, wfirst, preferred_element_type=jnp.float32
        ) + bias_first.astype(jnp.float32)
        activated = jax.nn.gelu(pre_act, approximate=False).astype(jnp.bfloat16)
        mlp_out = jnp.dot(activated, wsecond, preferred_element_type=jnp.float32) + biases[3]
        saved_acts.append(
            (
                residual,
                window_rows,
                queries,
                key_rows,
                values,
                log_total,
                mixed_rows,
                middle,
                normed_mlp,
                pre_act,
                activated,
            )
        )
        residual = middle + mlp_out.reshape(middle.shape)
    images_out = residual.astype(jnp.bfloat16)
    upstream = cotangent.astype(jnp.float32)
    layer_grads = [None] * layer_count
    table_list = [None] * layer_count
    for layer_num in reversed(range(layer_count)):
        shifted = layer_num % 2 == 1
        (
            residual_in,
            window_rows,
            queries,
            key_rows,
            values,
            log_total,
            mixed_rows,
            middle,
            normed_mlp,
            pre_act,
            activated,
        ) = saved_acts[layer_num]
        wqkv, wproj, gains, shifts, biases = (
            lax.all_gather(w_qkv[layer_num], "shard", axis=0, tiled=True),
            lax.all_gather(w_proj[layer_num], "shard", axis=0, tiled=True),
            lax.all_gather(norm_gains[layer_num], "shard", axis=1, tiled=True),
            lax.all_gather(norm_shifts[layer_num], "shard", axis=1, tiled=True),
            lax.all_gather(branch_biases[layer_num], "shard", axis=1, tiled=True),
        )
        wfirst, wsecond, bias_first = (
            lax.all_gather(w_fc1[layer_num], "shard", axis=0, tiled=True),
            lax.all_gather(w_fc2[layer_num], "shard", axis=0, tiled=True),
            lax.all_gather(fc1_bias[layer_num], "shard", axis=0, tiled=True),
        )
        gains = gains.astype(jnp.float32)
        shifts = shifts.astype(jnp.float32)
        out_grad = upstream.astype(jnp.bfloat16).reshape(-1, model_width)
        grad_b_second = jnp.sum(out_grad.astype(jnp.float32), axis=0)
        grad_w_second = transposed_times(activated, out_grad)
        act_grad = times_transposed(out_grad, wsecond)
        pre_grad = (act_grad * gelu_slope(pre_act)).astype(jnp.bfloat16)
        grad_b_first = jnp.sum(pre_grad.astype(jnp.float32), axis=0)
        grad_w_first = transposed_times(normed_mlp, pre_grad)
        norm_grad = times_transposed(pre_grad, wfirst).reshape(middle.shape)
        norm_pull = jax.vjp(layer_norm, middle, gains[1], shifts[1])[1]
        middle_part, grad_gain_mlp, grad_shift_mlp = norm_pull(norm_grad)
        middle_grad = upstream + middle_part
        branch_grad = middle_grad
        if shifted:
            branch_grad = jnp.roll(branch_grad, (-SHIFT, -SHIFT), axis=(1, 2))
        branch_rows = to_windows(branch_grad.astype(jnp.bfloat16)).reshape(tokens, model_width)
        grad_b_proj = jnp.sum(branch_rows.astype(jnp.float32), axis=0)
        grad_w_proj = transposed_times(mixed_rows, branch_rows)
        mixed_grad = heads_of(times_transposed(branch_rows, wproj).astype(jnp.bfloat16))
        scores = jnp.einsum(
            "nqhd,nkhd->nhqk", queries, key_rows, preferred_element_type=jnp.float32
        ) + score_bias(layer_num)
        attn_probs = jnp.exp(scores - log_total)
        prob_grad = jnp.einsum(
            "nqhd,nkhd->nhqk", mixed_grad, values, preferred_element_type=jnp.float32
        )
        value_grad = jnp.einsum(
            "nhqk,nqhd->nkhd",
            attn_probs.astype(jnp.bfloat16),
            mixed_grad,
            preferred_element_type=jnp.float32,
        ).astype(jnp.bfloat16)
        score_grad = (
            attn_probs * (prob_grad - jnp.sum(attn_probs * prob_grad, axis=-1, keepdims=True))
        ).astype(jnp.bfloat16)
        table_term = jnp.sum(score_grad.astype(jnp.float32), axis=0).reshape(head_count, -1).T
        table_list[layer_num] = jnp.dot(onehot.T, table_term, precision=highest)
        query_grad = jnp.einsum(
            "nhqk,nkhd->nqhd", score_grad, key_rows, preferred_element_type=jnp.float32
        ).astype(jnp.bfloat16)
        key_grad = jnp.einsum(
            "nhqk,nqhd->nkhd", score_grad, queries, preferred_element_type=jnp.float32
        ).astype(jnp.bfloat16)
        qkv_grad = jnp.concatenate(
            [
                query_grad.reshape(tokens, model_width),
                key_grad.reshape(tokens, model_width),
                value_grad.reshape(tokens, model_width),
            ],
            axis=1,
        )
        grad_w_proj_qkv = transposed_times(window_rows, qkv_grad) * column_scale[None, :]
        grad_b_query = (
            jnp.sum(query_grad.reshape(tokens, model_width).astype(jnp.float32), axis=0)
            * query_scale
        )
        grad_b_value = jnp.sum(value_grad.reshape(tokens, model_width).astype(jnp.float32), axis=0)
        rows_grad = times_transposed(qkv_grad[:, :model_width], wqkv[:, :model_width]) * query_scale
        rows_grad = rows_grad + times_transposed(qkv_grad[:, model_width:], wqkv[:, model_width:])
        normed_grad = from_windows(
            rows_grad.reshape(window_count, WIN * WIN, model_width), image_count
        )
        if shifted:
            normed_grad = jnp.roll(normed_grad, (SHIFT, SHIFT), axis=(1, 2))
        first_pull = jax.vjp(layer_norm, residual_in, gains[0], shifts[0])[1]
        input_part, grad_gain_attn, grad_shift_attn = first_pull(normed_grad)
        upstream = middle_grad + input_part
        gain_grads = jnp.stack([grad_gain_attn, grad_gain_mlp])
        shift_grads = jnp.stack([grad_shift_attn, grad_shift_mlp])
        bias_grads = jnp.stack([grad_b_query, grad_b_value, grad_b_proj, grad_b_second])
        qkv_share, proj_share, gain_share, shift_share, bias_share = (
            lax.psum_scatter(
                grad_w_proj_qkv.astype(jnp.bfloat16), "shard", scatter_dimension=0, tiled=True
            ).astype(jnp.float32),
            lax.psum_scatter(
                grad_w_proj.astype(jnp.bfloat16), "shard", scatter_dimension=0, tiled=True
            ).astype(jnp.float32),
            lax.psum_scatter(
                gain_grads.astype(jnp.bfloat16), "shard", scatter_dimension=1, tiled=True
            ).astype(jnp.float32),
            lax.psum_scatter(
                shift_grads.astype(jnp.bfloat16), "shard", scatter_dimension=1, tiled=True
            ).astype(jnp.float32),
            lax.psum_scatter(
                bias_grads.astype(jnp.bfloat16), "shard", scatter_dimension=1, tiled=True
            ).astype(jnp.float32),
        )
        first_share, second_share, bfirst_share = (
            lax.psum_scatter(
                grad_w_first.astype(jnp.bfloat16), "shard", scatter_dimension=0, tiled=True
            ).astype(jnp.float32),
            lax.psum_scatter(
                grad_w_second.astype(jnp.bfloat16), "shard", scatter_dimension=0, tiled=True
            ).astype(jnp.float32),
            lax.psum_scatter(
                grad_b_first.astype(jnp.bfloat16), "shard", scatter_dimension=0, tiled=True
            ).astype(jnp.float32),
        )
        layer_grads[layer_num] = (
            qkv_share,
            proj_share,
            first_share,
            second_share,
            gain_share,
            shift_share,
            bias_share,
            bfirst_share,
        )
    stacked = [jnp.stack([layer_grads[n][m] for n in range(layer_count)]) for m in range(8)]
    summed = replica_total(stacked)
    table_total = lax.psum(jnp.stack(table_list), ("rep", "shard"))
    return (
        images_out,
        upstream,
        summed[0],
        summed[1],
        summed[2],
        summed[3],
        summed[4],
        summed[5],
        summed[6],
        summed[7],
        table_total,
    )


def solution(mesh):
    return jax.shard_map(
        body,
        mesh=mesh,
        in_specs=(
            P(("rep", "shard"), None, None, None),
            P(("rep", "shard"), None, None, None),
            P(("rep", "shard"), None, None),
            P(None, "shard", None),
            P(None, "shard", None),
            P(None, "shard", None),
            P(None, "shard", None),
            P(None, None, "shard"),
            P(None, None, "shard"),
            P(None, None, "shard"),
            P(None, "shard"),
            P(),
        ),
        out_specs=(
            P(("rep", "shard"), None, None, None),
            P(("rep", "shard"), None, None, None),
            P(None, "shard", None),
            P(None, "shard", None),
            P(None, "shard", None),
            P(None, "shard", None),
            P(None, None, "shard"),
            P(None, None, "shard"),
            P(None, None, "shard"),
            P(None, "shard"),
            P(),
        ),
        check_vma=False,
    )
```

profile of v0, /device:TPU:0, one launch (start us, length us, event | category | flops | bytes accessed | tf_op | source)
XLA Modules:
  0.0 1341.8 jit_solution(16533433941194631323)
XLA Ops:
  17.5 24.0 %all-gather = bf16[1,2,512]{1,0,2:T(2,128)(2,1)S(1)} all-gather(bf16[1,2,32]{1,0,2:T(2,128)(2,1)S(1)} %copy.412), channel_id=2, replica_groups=mesh['rep'=2,'shard'=16] {'shard'}, dimensions={2}, use_global_device_ids=true | all-gather | bytes 2176 | tf_op jit(solution)/shard_map/all_gather | solution.py:134
  44.6 18.3 %all-gather.1 = bf16[1,2,512]{1,0,2:T(2,128)(2,1)S(1)} all-gather(bf16[1,2,32]{1,0,2:T(2,128)(2,1)S(1)} %copy.413), channel_id=3, replica_groups=mesh['rep'=2,'shard'=16] {'shard'}, dimensions={2}, use_global_device_ids=true | all-gather | bytes 2176 | tf_op jit(solution)/shard_map/all_gather | solution.py:135
  67.9 20.7 %all-gather.3 = bf16[1,4,512]{1,0,2:T(2,128)(2,1)S(1)} all-gather(bf16[1,4,32]{1,0,2:T(2,128)(2,1)S(1)} %copy.414), channel_id=5, replica_groups=mesh['rep'=2,'shard'=16] {'shard'}, dimensions={2}, use_global_device_ids=true | all-gather | bytes 4352 | tf_op jit(solution)/shard_map/all_gather | solution.py:136
  96.1 19.4 %all-gather.4 = bf16[1,512,512]{2,1,0:T(8,128)(2,1)S(1)} all-gather(bf16[1,32,512]{2,1,0:T(8,128)(2,1)S(1)} %get-tuple-element.155), channel_id=6, replica_groups=mesh['rep'=2,'shard'=16] {'shard'}, dimensions={1}, use_global_device_ids=true | all-gather | bytes 557056 | tf_op jit(solution)/shard_map/all_gather | solution.py:133
  115.5 18.6 %all-gather.6 = bf16[1,2048]{1,0:T(2,128)(2,1)S(1)} all-gather(bf16[1,128]{1,0:T(2,128)(2,1)S(1)} %get-tuple-element.163), channel_id=8, replica_groups=mesh['rep'=2,'shard'=16] {'shard'}, dimensions={1}, use_global_device_ids=true | all-gather | bytes 4352 | tf_op jit(solution)/shard_map/all_gather | solution.py:141
  134.3 18.2 %all-gather.8 = bf16[1,2,512]{1,0,2:T(2,128)(2,1)S(1)} all-gather(bf16[1,2,32]{1,0,2:T(2,128)(2,1)S(1)} %copy.415), channel_id=10, replica_groups=mesh['rep'=2,'shard'=16] {'shard'}, dimensions={2}, use_global_device_ids=true | all-gather | bytes 2176 | tf_op jit(solution)/shard_map/all_gather | solution.py:134
  156.2 19.6 %all-gather.9 = bf16[1,2,512]{1,0,2:T(2,128)(2,1)S(1)} all-gather(bf16[1,2,32]{1,0,2:T(2,128)(2,1)S(1)} %copy.416), channel_id=11, replica_groups=mesh['rep'=2,'shard'=16] {'shard'}, dimensions={2}, use_global_device_ids=true | all-gather | bytes 2176 | tf_op jit(solution)/shard_map/all_gather | solution.py:135
  179.4 31.4 %all-gather.11 = bf16[1,4,512]{1,0,2:T(2,128)(2,1)S(1)} all-gather(bf16[1,4,32]{1,0,2:T(2,128)(2,1)S(1)} %copy.417), channel_id=13, replica_groups=mesh['rep'=2,'shard'=16] {'shard'}, dimensions={2}, use_global_device_ids=true | all-gather | bytes 4352 | tf_op jit(solution)/shard_map/all_gather | solution.py:136
  220.6 21.8 %all-gather.12 = bf16[1,512,512]{2,1,0:T(8,128)(2,1)} all-gather(bf16[1,32,512]{2,1,0:T(8,128)(2,1)S(1)} %get-tuple-element.154), channel_id=14, replica_groups=mesh['rep'=2,'shard'=16] {'shard'}, dimensions={1}, use_global_device_ids=true | all-gather | bytes 557056 | tf_op jit(solution)/shard_map/all_gather | solution.py:133
  497.7 31.7 %all-reduce.2 = (bf16[2048]{0:T(1024)(128)(2,1)S(1)}, bf16[2048]{0:T(1024)(128)(2,1)S(1)}) all-reduce(bf16[2048]{0:T(1024)(128)(2,1)S(1)} %copy-done.107, bf16[2048]{0:T(1024)(128)(2,1)S(1)} %copy-done.108), channel_id=33, replica_groups=mesh['rep'=2,'shard'=16] {'shard'}, use_global_device_ids=true, to_apply=%region_63.64.clone | all-reduce | flops 4096 | bytes 16384
  534.4 37.7 %psum.71 = f32[2,169,16]{1,2,0:T(8,128)} all-reduce(f32[2,169,16]{1,2,0:T(8,128)S(1)} %pad_maximum_fusion.10), channel_id=1, replica_groups=mesh['rep'=2,'shard'=16] {'rep','shard'}, use_global_device_ids=true, to_apply=%region_67.68 | all-reduce | flops 5408 | bytes 43264 | tf_op jit(solution)/shard_map/psum | solution.py:340
  573.6 53.1 %reduce-scatter.27.cloned.1.call-done = bf16[32,1536]{1,0:T(8,128)(2,1)} async-done(((bf16[512,1536]{1,0:T(8,128)(2,1)}), bf16[32,1536]{1,0:T(8,128)(2,1)}) %reduce-scatter.27.cloned.1.call-update) | async-done | bytes 98320 | tf_op jit(solution)/shard_map/reduce_scatter | solution.py:301
  626.7 62.5 %reduce-scatter.29.cloned.1.call-done = bf16[32,1536]{1,0:T(8,128)(2,1)} async-done(((bf16[512,1536]{1,0:T(8,128)(2,1)}), bf16[32,1536]{1,0:T(8,128)(2,1)}) %reduce-scatter.29.cloned.1.call-update) | async-done | bytes 98320 | tf_op jit(solution)/shard_map/reduce_scatter | solution.py:301
  690.8 62.7 %reduce-scatter.37.cloned.1.call-done = bf16[32,2048]{1,0:T(8,128)(2,1)} async-done(((bf16[512,2048]{1,0:T(8,128)(2,1)}), bf16[32,2048]{1,0:T(8,128)(2,1)}) %reduce-scatter.37.cloned.1.call-update) | async-done | bytes 131088 | tf_op jit(solution)/shard_map/reduce_scatter | solution.py:318
  753.6 64.6 %reduce-scatter.35.cloned.1.call-done = bf16[32,2048]{1,0:T(8,128)(2,1)} async-done(((bf16[512,2048]{1,0:T(8,128)(2,1)}), bf16[32,2048]{1,0:T(8,128)(2,1)}) %reduce-scatter.35.cloned.1.call-update) | async-done | bytes 131088 | tf_op jit(solution)/shard_map/reduce_scatter | solution.py:318
  819.9 62.6 %reduce-scatter.39.cloned.1.call-done = bf16[128,512]{1,0:T(8,128)(2,1)} async-done(((bf16[2048,512]{1,0:T(8,128)(2,1)}), bf16[128,512]{1,0:T(8,128)(2,1)}) %reduce-scatter.39.cloned.1.call-update) | async-done | bytes 131088 | tf_op jit(solution)/shard_map/reduce_scatter | solution.py:321
  882.4 64.7 %reduce-scatter.41.cloned.1.call-done = bf16[128,512]{1,0:T(8,128)(2,1)} async-done(((bf16[2048,512]{1,0:T(8,128)(2,1)}), bf16[128,512]{1,0:T(8,128)(2,1)}) %reduce-scatter.41.cloned.1.call-update) | async-done | bytes 131088 | tf_op jit(solution)/shard_map/reduce_scatter | solution.py:321
  950.1 54.4 %reduce-scatter.47.cloned.1.call-done = bf16[32,2]{1,0:T(8,128)(2,1)} async-done(((bf16[512,2]{1,0:T(8,128)(2,1)}), bf16[32,2]{1,0:T(8,128)(2,1)}) %reduce-scatter.47.cloned.1.call-update) | async-done | bytes 144
  1005.3 56.7 %reduce-scatter.49.cloned.1.call-done = bf16[32,2]{1,0:T(8,128)(2,1)} async-done(((bf16[512,2]{1,0:T(8,128)(2,1)}), bf16[32,2]{1,0:T(8,128)(2,1)}) %reduce-scatter.49.cloned.1.call-update) | async-done | bytes 144
  1062.8 56.7 %reduce-scatter.43.cloned.1.call-done = bf16[32,2]{1,0:T(8,128)(2,1)} async-done(((bf16[512,2]{1,0:T(8,128)(2,1)}), bf16[32,2]{1,0:T(8,128)(2,1)}) %reduce-scatter.43.cloned.1.call-update) | async-done | bytes 144
  1120.2 57.2 %reduce-scatter.45.cloned.1.call-done = bf16[32,2]{1,0:T(8,128)(2,1)} async-done(((bf16[512,2]{1,0:T(8,128)(2,1)}), bf16[32,2]{1,0:T(8,128)(2,1)}) %reduce-scatter.45.cloned.1.call-update) | async-done | bytes 144
  1178.3 56.8 %reduce-scatter.51.cloned.1.call-done = bf16[32,4]{1,0:T(8,128)(2,1)} async-done(((bf16[512,4]{1,0:T(8,128)(2,1)}), bf16[32,4]{1,0:T(8,128)(2,1)}) %reduce-scatter.51.cloned.1.call-update) | async-done | bytes 272
  1235.8 56.7 %reduce-scatter.53.cloned.1.call-done = bf16[32,4]{1,0:T(8,128)(2,1)} async-done(((bf16[512,4]{1,0:T(8,128)(2,1)}), bf16[32,4]{1,0:T(8,128)(2,1)}) %reduce-scatter.53.cloned.1.call-update) | async-done | bytes 272
  1300.6 28.8 %all-reduce.7.cloned.1.call-done = (bf16[2,32,1536]{2,1,0:T(8,128)(2,1)}, bf16[2,32,512]{2,1,0:T(8,128)(2,1)}, bf16[2,32,2048]{2,1,0:T(8,128)(2,1)}, bf16[2,128,512]{2,1,0:T(8,128)(2,1)}) async-done(((bf16[2,32,1536]{2,1,0:T(8,128)(2,1)}, bf16[2,32,512]{2,1,0:T(8,128)(2,1)}, bf16[2,32,2048]{2,1,0:T(8,128)(2,1)}, bf16[2,128,512]{2,1,0:T(8,128)(2,1)}), (bf16[2,32,1536]{2,1,0:T(8,128)(2,1)}, ...) | async-done | bytes 786448 | tf_op jit(solution)/shard_map/psum | solution.py:71
  (556 shorter events, 325.5 us)
Async XLA Ops:
  7.2 253.9 %all-gather.23.cloned.1.call-start = ((), (), s32[]{:S(2)}) async-start(), calls=%async_computation.22 | async-start | bytes 1671168 | tf_op jit(solution)/shard_map/all_gather | solution.py:132
  8.9 275.0 %all-gather.25.cloned.1.call-start = ((), (), s32[]{:S(2)}) async-start(), calls=%async_computation.23 | async-start | bytes 2228224 | tf_op jit(solution)/shard_map/all_gather | solution.py:139
  10.7 280.6 %all-gather.27.cloned.1.call-start = ((), (), s32[]{:S(2)}) async-start(), calls=%async_computation.24 | async-start | bytes 2228224 | tf_op jit(solution)/shard_map/all_gather | solution.py:140
  12.4 288.5 %all-gather.29.cloned.1.call-start = ((), (), s32[]{:S(2)}) async-start(), calls=%async_computation.25 | async-start | bytes 1671168 | tf_op jit(solution)/shard_map/all_gather | solution.py:132
  13.0 321.2 %all-gather.31.cloned.1.call-start = ((), (), s32[]{:S(2)}) async-start(), calls=%async_computation.26 | async-start | bytes 2228224 | tf_op jit(solution)/shard_map/all_gather | solution.py:139
  13.6 327.7 %all-gather.33.cloned.1.call-start = ((), (), s32[]{:S(2)}) async-start(), calls=%async_computation.27 | async-start | bytes 2228224 | tf_op jit(solution)/shard_map/all_gather | solution.py:140
  14.2 558.0 %reduce-scatter.33.cloned.1.call-start = ((), (), s32[]{:S(2)}) async-start(), calls=%async_computation.17 | async-start | bytes 557056 | tf_op jit(solution)/shard_map/reduce_scatter | solution.py:304
  44.5 238.0 %copy-start.81 = (f32[512]{0:T(512)}, f32[512]{0:T(512)S(1)}, u32[]{:S(2)}) copy-start(f32[512]{0:T(512)S(1)} %get-tuple-element.101) | copy-start | bytes 6148
  67.8 193.3 %copy-start.39 = (bf16[196,512]{1,0:T(8,128)(2,1)}, bf16[196,512]{1,0:T(8,128)(2,1)S(1)}, u32[]{:S(2)}) copy-start(bf16[196,512]{1,0:T(8,128)(2,1)S(1)} %reshape_reshape.24) | copy-start | bytes 602116
  450.9 121.3 %reduce-scatter.31.cloned.1.call-start = ((), (), s32[]{:S(2)}) async-start(), calls=%async_computation.16 | async-start | bytes 557056 | tf_op jit(solution)/shard_map/reduce_scatter | solution.py:304
  460.2 166.5 %reduce-scatter.27.cloned.1.call-start = ((), (), s32[]{:S(2)}) async-start(), calls=%async_computation.14 | async-start | bytes 1671168 | tf_op jit(solution)/shard_map/reduce_scatter | solution.py:301
  466.2 223.0 %reduce-scatter.29.cloned.1.call-start = ((), (), s32[]{:S(2)}) async-start(), calls=%async_computation.15 | async-start | bytes 1671168 | tf_op jit(solution)/shard_map/reduce_scatter | solution.py:301
  468.1 285.4 %reduce-scatter.37.cloned.1.call-start = ((), (), s32[]{:S(2)}) async-start(), calls=%async_computation.19 | async-start | bytes 2228224 | tf_op jit(solution)/shard_map/reduce_scatter | solution.py:318
  471.4 346.8 %reduce-scatter.35.cloned.1.call-start = ((), (), s32[]{:S(2)}) async-start(), calls=%async_computation.18 | async-start | bytes 2228224 | tf_op jit(solution)/shard_map/reduce_scatter | solution.py:318
  474.6 407.8 %reduce-scatter.39.cloned.1.call-start = ((), (), s32[]{:S(2)}) async-start(), calls=%async_computation.20 | async-start | bytes 2228224 | tf_op jit(solution)/shard_map/reduce_scatter | solution.py:321
  478.0 469.1 %reduce-scatter.41.cloned.1.call-start = ((), (), s32[]{:S(2)}) async-start(), calls=%async_computation.21 | async-start | bytes 2228224 | tf_op jit(solution)/shard_map/reduce_scatter | solution.py:321
  481.4 523.2 %reduce-scatter.47.cloned.1.call-start = ((), (), s32[]{:S(2)}) async-start(), calls=%async_computation.30 | async-start | bytes 139264
  496.8 565.2 %reduce-scatter.49.cloned.1.call-start = ((), (), s32[]{:S(2)}) async-start(), calls=%async_computation.31 | async-start | bytes 139264
  529.4 590.0 %reduce-scatter.43.cloned.1.call-start = ((), (), s32[]{:S(2)}) async-start(), calls=%async_computation.28 | async-start | bytes 139264
  530.4 647.1 %reduce-scatter.45.cloned.1.call-start = ((), (), s32[]{:S(2)}) async-start(), calls=%async_computation.29 | async-start | bytes 139264
  531.8 703.2 %reduce-scatter.51.cloned.1.call-start = ((), (), s32[]{:S(2)}) async-start(), calls=%async_computation.32 | async-start | bytes 139264
  533.6 415.3 %copy-start.34 = (f32[1,14,14,512]{3,0,2,1:T(1,128)S(1)}, f32[1,14,14,512]{3,0,2,1:T(1,128)}, u32[]{:S(2)}) copy-start(f32[1,14,14,512]{3,0,2,1:T(1,128)} %get-tuple-element.127) | copy-start | bytes 1204228
  534.3 758.2 %reduce-scatter.53.cloned.1.call-start = ((), (), s32[]{:S(2)}) async-start(), calls=%async_computation.33 | async-start | bytes 139264
  572.1 757.3 %all-reduce.7.cloned.1.call-start = ((), (), s32[]{:S(2)}) async-start(), calls=%async_computation.34 | async-start | bytes 1572864 | tf_op jit(solution)/shard_map/psum | solution.py:71
  (113 other events, 1343.8 us)
Sparse Core Ops, SparseCore 0:
  10.9 42.7 all-gather.22
  56.4 40.3 all-gather.24
  99.5 40.4 all-gather.26
  142.1 38.9 all-gather.28
  183.7 40.5 all-gather.30
  226.9 40.4 all-gather.32
  451.1 53.9 reduce-scatter.32
  509.6 54.7 reduce-scatter.30
  568.1 58.5 reduce-scatter.26
  630.6 58.4 reduce-scatter.28
  692.9 60.5 reduce-scatter.36
  757.6 60.5 reduce-scatter.34
  821.9 60.4 reduce-scatter.38
  886.5 60.5 reduce-scatter.40
  950.4 54.0 reduce-scatter.46
  1007.8 54.1 reduce-scatter.48
  1065.3 54.0 reduce-scatter.42
  1123.3 54.0 reduce-scatter.44
  1180.9 54.0 reduce-scatter.50
  1238.3 54.0 reduce-scatter.52
  1295.5 33.8 all-reduce.6
where the time goes:
time: 1350 us; the launch traced here: 1340 us
  waiting for transfers between devices  739 us (55%)
  blocking collectives  284 us (21%)
  local copies, waits for them, and re-layouts  132 us (10%)
  other arithmetic  84.2 us (6%)
  matrix products  84.1 us (6%)
  between operations  17.4 us (1%)
    unnamed x27, waiting for transfers between devices  340 us
    reduce_scatter x2, waiting for transfers between devices, body(): lax.psum_scatter(grad_w_first.astype(jnp.bfloat16), 'shard', scatter_dime...  127 us
    reduce_scatter x2, waiting for transfers between devices, body(): lax.psum_scatter(grad_w_second.astype(jnp.bfloat16), 'shard', scatter_dim...  127 us
    reduce_scatter x2, waiting for transfers between devices, body(): lax.psum_scatter(grad_w_proj_qkv.astype(jnp.bfloat16), 'shard', scatter_d...  116 us
    all_gather x2, blocking collectives, body(): lax.all_gather(branch_biases[layer_num], 'shard', axis=1, tiled=True)  52.1 us
    all_gather x2, blocking collectives, body(): lax.all_gather(norm_gains[layer_num], 'shard', axis=1, tiled=True)  42.1 us
    all_gather x2, blocking collectives, body(): lax.all_gather(w_proj[layer_num], 'shard', axis=0, tiled=True)  41.2 us
    all_gather x2, blocking collectives, body(): lax.all_gather(norm_shifts[layer_num], 'shard', axis=1, tiled=True)  37.8 us
  transfers between devices with their start and end apart: 21, of which 13 were waited for; matrix products, arithmetic and copies ran while one was open for 13% of the time, Pallas kernels for 0%

commit v1 on v0

--- a/solution.py
+++ b/solution.py
@@ -10,6 +10,34 @@
 highest = lax.Precision.HIGHEST
 inv_root_two = 0.7071067811865476
 inv_root_two_pi = 0.3989422804014327
+
+
+def _see_rows(payload, peer_axis):
+    e_now = lax.axis_size(peer_axis)
+    state_now, top, r_now = (e_now, lax.axis_index(peer_axis), payload.shape[0])
+    found = []
+    for hop_no, k0 in enumerate(payload.shape):
+        found.append(k0 * state_now if hop_no == 0 else k0)
+    view_out = jnp.zeros(found, payload.dtype)
+    answer = lax.dynamic_update_slice_in_dim(view_out, payload, top * r_now, axis=0)
+    carry_in = s_next = payload
+    for h in [*range(1, state_now // 2 + 1)]:
+        gallery = []
+        for hop_no in tuple(range(state_now)):
+            gallery.append((hop_no, (hop_no + 1) % state_now))
+        carry_in = lax.ppermute(carry_in, axis_name=peer_axis, perm=gallery)
+        answer = lax.dynamic_update_slice_in_dim(
+            answer, carry_in, (top - h) % state_now * r_now, axis=0
+        )
+        if 2 * h < state_now:
+            arrivals = []
+            for hop_no in tuple(range(state_now)):
+                arrivals.append((hop_no, (hop_no - 1) % state_now))
+            s_next = lax.ppermute(s_next, axis_name=peer_axis, perm=arrivals)
+            answer = lax.dynamic_update_slice_in_dim(
+                answer, s_next, (top + h) % state_now * r_now, axis=0
+            )
+    return answer
 
 
 def layer_norm(values, norm_gain, norm_shift):
@@ -138,7 +166,7 @@
         mlp_w = (
             lax.all_gather(w_fc1[layer_num], "shard", axis=0, tiled=True),
             lax.all_gather(w_fc2[layer_num], "shard", axis=0, tiled=True),
-            lax.all_gather(fc1_bias[layer_num], "shard", axis=0, tiled=True),
+            _see_rows(fc1_bias[layer_num], "shard"),
         )
         kept_weights.append((attn_w, mlp_w))
         wqkv, wproj, gains, shifts, biases = attn_w

time: 1350 us -> 1370 us (1.015)
  starting transfers between devices: 1.33 us -> 64.7 us
  blocking collectives: 284 us -> 231 us
    ppermute x0 -> x30, starting transfers between devices: none -> 63.3 us  [the longest x14 62.2 us: _see_rows(): s_next = lax.ppermute(s_next, axis_name=peer_axis, perm=arrivals)]
    all_gather x2 -> x0, blocking collectives: 36 us -> none  [body(): lax.all_gather(fc1_bias[layer_num], 'shard', axis=0, tiled=True)]
    all_gather x2, blocking collectives: 52.1 us -> 37.8 us  [body(): lax.all_gather(branch_biases[layer_num], 'shard', axis=1, tiled=True)]
  transfers between devices with their start and end apart: 21 -> 51, of which waited for: 13 -> 16; matrix products, arithmetic and copies ran while one was open for 13% -> 13% of each run, Pallas kernels for 0% -> 0%
where the time goes in v1:
time: 1370 us; the launch traced here: 1360 us
  waiting for transfers between devices  744 us (54%)
  blocking collectives  231 us (17%)
  local copies, waits for them, and re-layouts  138 us (10%)
  matrix products  84.6 us (6%)
  other arithmetic  84 us (6%)
  starting transfers between devices  64.7 us (5%)
  between operations  17.6 us (1%)
    unnamed x27, waiting for transfers between devices  340 us
    reduce_scatter x2, waiting for transfers between devices, body(): lax.psum_scatter(grad_w_first.astype(jnp.bfloat16), 'shard', scatter_dime...  127 us
    reduce_scatter x2, waiting for transfers between devices, body(): lax.psum_scatter(grad_w_second.astype(jnp.bfloat16), 'shard', scatter_dim...  127 us
    reduce_scatter x2, waiting for transfers between devices, body(): lax.psum_scatter(grad_w_proj_qkv.astype(jnp.bfloat16), 'shard', scatter_d...  116 us
    ppermute x14, starting transfers between devices, _see_rows(): s_next = lax.ppermute(s_next, axis_name=peer_axis, perm=arrivals)  62.2 us
    all_gather x2, blocking collectives, body(): lax.all_gather(w_proj[layer_num], 'shard', axis=0, tiled=True)  43.8 us
    all_gather x2, blocking collectives, body(): lax.all_gather(norm_shifts[layer_num], 'shard', axis=1, tiled=True)  40.1 us
    all_gather x2, blocking collectives, body(): lax.all_gather(branch_biases[layer_num], 'shard', axis=1, tiled=True)  37.8 us
  transfers between devices with their start and end apart: 51, of which 16 were waited for; matrix products, arithmetic and copies ran while one was open for 13% of the time, Pallas kernels for 0%

profile of v1, /device:TPU:0, one launch (start us, length us, event | category | flops | bytes accessed | tf_op | source)
XLA Modules:
  0.0 1364.6 jit_solution(8623569379943190570)
XLA Ops:
  27.3 18.0 %all-gather = bf16[1,2,512]{1,0,2:T(2,128)(2,1)S(1)} all-gather(bf16[1,2,32]{1,0,2:T(2,128)(2,1)S(1)} %copy.412), channel_id=2, replica_groups=mesh['rep'=2,'shard'=16] {'shard'}, dimensions={2}, use_global_device_ids=true | all-gather | bytes 2176 | tf_op jit(solution)/shard_map/all_gather | solution.py:162
  48.5 20.2 %all-gather.1 = bf16[1,2,512]{1,0,2:T(2,128)(2,1)S(1)} all-gather(bf16[1,2,32]{1,0,2:T(2,128)(2,1)S(1)} %copy.413), channel_id=3, replica_groups=mesh['rep'=2,'shard'=16] {'shard'}, dimensions={2}, use_global_device_ids=true | all-gather | bytes 2176 | tf_op jit(solution)/shard_map/all_gather | solution.py:163
  73.7 18.9 %all-gather.3 = bf16[1,4,512]{1,0,2:T(2,128)(2,1)S(1)} all-gather(bf16[1,4,32]{1,0,2:T(2,128)(2,1)S(1)} %copy.414), channel_id=5, replica_groups=mesh['rep'=2,'shard'=16] {'shard'}, dimensions={2}, use_global_device_ids=true | all-gather | bytes 4352 | tf_op jit(solution)/shard_map/all_gather | solution.py:164
  100.2 21.6 %all-gather.4 = bf16[1,512,512]{2,1,0:T(8,128)(2,1)S(1)} all-gather(bf16[1,32,512]{2,1,0:T(8,128)(2,1)S(1)} %get-tuple-element.155), channel_id=6, replica_groups=mesh['rep'=2,'shard'=16] {'shard'}, dimensions={1}, use_global_device_ids=true | all-gather | bytes 557056 | tf_op jit(solution)/shard_map/all_gather | solution.py:161
  121.8 18.5 %all-gather.7 = bf16[1,2,512]{1,0,2:T(2,128)(2,1)S(1)} all-gather(bf16[1,2,32]{1,0,2:T(2,128)(2,1)S(1)} %copy.415), channel_id=9, replica_groups=mesh['rep'=2,'shard'=16] {'shard'}, dimensions={2}, use_global_device_ids=true | all-gather | bytes 2176 | tf_op jit(solution)/shard_map/all_gather | solution.py:162
  144.0 19.9 %all-gather.8 = bf16[1,2,512]{1,0,2:T(2,128)(2,1)S(1)} all-gather(bf16[1,2,32]{1,0,2:T(2,128)(2,1)S(1)} %copy.416), channel_id=10, replica_groups=mesh['rep'=2,'shard'=16] {'shard'}, dimensions={2}, use_global_device_ids=true | all-gather | bytes 2176 | tf_op jit(solution)/shard_map/all_gather | solution.py:163
  167.6 18.9 %all-gather.10 = bf16[1,4,512]{1,0,2:T(2,128)(2,1)S(1)} all-gather(bf16[1,4,32]{1,0,2:T(2,128)(2,1)S(1)} %copy.417), channel_id=12, replica_groups=mesh['rep'=2,'shard'=16] {'shard'}, dimensions={2}, use_global_device_ids=true | all-gather | bytes 4352 | tf_op jit(solution)/shard_map/all_gather | solution.py:164
  186.8 7.3 slice_reduce_fusion
  196.2 22.3 %all-gather.11 = bf16[1,512,512]{2,1,0:T(8,128)(2,1)} all-gather(bf16[1,32,512]{2,1,0:T(8,128)(2,1)S(1)} %get-tuple-element.154), channel_id=13, replica_groups=mesh['rep'=2,'shard'=16] {'shard'}, dimensions={1}, use_global_device_ids=true | all-gather | bytes 557056 | tf_op jit(solution)/shard_map/all_gather | solution.py:161
  522.0 30.0 %all-reduce.2 = (bf16[2048]{0:T(1024)(128)(2,1)S(1)}, bf16[2048]{0:T(1024)(128)(2,1)S(1)}) all-reduce(bf16[2048]{0:T(1024)(128)(2,1)S(1)} %copy-done.107, bf16[2048]{0:T(1024)(128)(2,1)S(1)} %copy-done.108), channel_id=31, replica_groups=mesh['rep'=2,'shard'=16] {'shard'}, use_global_device_ids=true, to_apply=%region_63.64.clone | all-reduce | flops 4096 | bytes 16384
  557.1 37.7 %psum.71 = f32[2,169,16]{1,2,0:T(8,128)} all-reduce(f32[2,169,16]{1,2,0:T(8,128)S(1)} %pad_maximum_fusion.10), channel_id=1, replica_groups=mesh['rep'=2,'shard'=16] {'rep','shard'}, use_global_device_ids=true, to_apply=%region_67.68 | all-reduce | flops 5408 | bytes 43264 | tf_op jit(solution)/shard_map/psum | solution.py:368
  596.3 53.3 %reduce-scatter.27.cloned.1.call-done = bf16[32,1536]{1,0:T(8,128)(2,1)} async-done(((bf16[512,1536]{1,0:T(8,128)(2,1)}), bf16[32,1536]{1,0:T(8,128)(2,1)}) %reduce-scatter.27.cloned.1.call-update) | async-done | bytes 98320 | tf_op jit(solution)/shard_map/reduce_scatter | solution.py:329
  649.5 62.5 %reduce-scatter.29.cloned.1.call-done = bf16[32,1536]{1,0:T(8,128)(2,1)} async-done(((bf16[512,1536]{1,0:T(8,128)(2,1)}), bf16[32,1536]{1,0:T(8,128)(2,1)}) %reduce-scatter.29.cloned.1.call-update) | async-done | bytes 98320 | tf_op jit(solution)/shard_map/reduce_scatter | solution.py:329
  713.7 62.8 %reduce-scatter.37.cloned.1.call-done = bf16[32,2048]{1,0:T(8,128)(2,1)} async-done(((bf16[512,2048]{1,0:T(8,128)(2,1)}), bf16[32,2048]{1,0:T(8,128)(2,1)}) %reduce-scatter.37.cloned.1.call-update) | async-done | bytes 131088 | tf_op jit(solution)/shard_map/reduce_scatter | solution.py:346
  776.4 64.7 %reduce-scatter.35.cloned.1.call-done = bf16[32,2048]{1,0:T(8,128)(2,1)} async-done(((bf16[512,2048]{1,0:T(8,128)(2,1)}), bf16[32,2048]{1,0:T(8,128)(2,1)}) %reduce-scatter.35.cloned.1.call-update) | async-done | bytes 131088 | tf_op jit(solution)/shard_map/reduce_scatter | solution.py:346
  842.8 62.7 %reduce-scatter.39.cloned.1.call-done = bf16[128,512]{1,0:T(8,128)(2,1)} async-done(((bf16[2048,512]{1,0:T(8,128)(2,1)}), bf16[128,512]{1,0:T(8,128)(2,1)}) %reduce-scatter.39.cloned.1.call-update) | async-done | bytes 131088 | tf_op jit(solution)/shard_map/reduce_scatter | solution.py:349
  905.4 64.7 %reduce-scatter.41.cloned.1.call-done = bf16[128,512]{1,0:T(8,128)(2,1)} async-done(((bf16[2048,512]{1,0:T(8,128)(2,1)}), bf16[128,512]{1,0:T(8,128)(2,1)}) %reduce-scatter.41.cloned.1.call-update) | async-done | bytes 131088 | tf_op jit(solution)/shard_map/reduce_scatter | solution.py:349
  973.1 54.5 %reduce-scatter.47.cloned.1.call-done = bf16[32,2]{1,0:T(8,128)(2,1)} async-done(((bf16[512,2]{1,0:T(8,128)(2,1)}), bf16[32,2]{1,0:T(8,128)(2,1)}) %reduce-scatter.47.cloned.1.call-update) | async-done | bytes 144
  1028.4 56.7 %reduce-scatter.49.cloned.1.call-done = bf16[32,2]{1,0:T(8,128)(2,1)} async-done(((bf16[512,2]{1,0:T(8,128)(2,1)}), bf16[32,2]{1,0:T(8,128)(2,1)}) %reduce-scatter.49.cloned.1.call-update) | async-done | bytes 144
  1085.8 56.6 %reduce-scatter.43.cloned.1.call-done = bf16[32,2]{1,0:T(8,128)(2,1)} async-done(((bf16[512,2]{1,0:T(8,128)(2,1)}), bf16[32,2]{1,0:T(8,128)(2,1)}) %reduce-scatter.43.cloned.1.call-update) | async-done | bytes 144
  1143.2 57.3 %reduce-scatter.45.cloned.1.call-done = bf16[32,2]{1,0:T(8,128)(2,1)} async-done(((bf16[512,2]{1,0:T(8,128)(2,1)}), bf16[32,2]{1,0:T(8,128)(2,1)}) %reduce-scatter.45.cloned.1.call-update) | async-done | bytes 144
  1201.3 56.8 %reduce-scatter.51.cloned.1.call-done = bf16[32,4]{1,0:T(8,128)(2,1)} async-done(((bf16[512,4]{1,0:T(8,128)(2,1)}), bf16[32,4]{1,0:T(8,128)(2,1)}) %reduce-scatter.51.cloned.1.call-update) | async-done | bytes 272
  1258.9 56.6 %reduce-scatter.53.cloned.1.call-done = bf16[32,4]{1,0:T(8,128)(2,1)} async-done(((bf16[512,4]{1,0:T(8,128)(2,1)}), bf16[32,4]{1,0:T(8,128)(2,1)}) %reduce-scatter.53.cloned.1.call-update) | async-done | bytes 272
  1323.6 28.9 %all-reduce.7.cloned.1.call-done = (bf16[2,32,1536]{2,1,0:T(8,128)(2,1)}, bf16[2,32,512]{2,1,0:T(8,128)(2,1)}, bf16[2,32,2048]{2,1,0:T(8,128)(2,1)}, bf16[2,128,512]{2,1,0:T(8,128)(2,1)}) async-done(((bf16[2,32,1536]{2,1,0:T(8,128)(2,1)}, bf16[2,32,512]{2,1,0:T(8,128)(2,1)}, bf16[2,32,2048]{2,1,0:T(8,128)(2,1)}, bf16[2,128,512]{2,1,0:T(8,128)(2,1)}), (bf16[2,32,1536]{2,1,0:T(8,128)(2,1)}, ...) | async-done | bytes 786448 | tf_op jit(solution)/shard_map/psum | solution.py:99
  (648 shorter events, 375.9 us)
Async XLA Ops:
  7.2 277.9 %all-gather.21.cloned.1.call-start = ((), (), s32[]{:S(2)}) async-start(), calls=%async_computation.22 | async-start | bytes 1671168 | tf_op jit(solution)/shard_map/all_gather | solution.py:160
  8.9 299.0 %all-gather.23.cloned.1.call-start = ((), (), s32[]{:S(2)}) async-start(), calls=%async_computation.23 | async-start | bytes 2228224 | tf_op jit(solution)/shard_map/all_gather | solution.py:167
  10.7 304.3 %all-gather.25.cloned.1.call-start = ((), (), s32[]{:S(2)}) async-start(), calls=%async_computation.24 | async-start | bytes 2228224 | tf_op jit(solution)/shard_map/all_gather | solution.py:168
  12.5 312.1 %all-gather.27.cloned.1.call-start = ((), (), s32[]{:S(2)}) async-start(), calls=%async_computation.25 | async-start | bytes 1671168 | tf_op jit(solution)/shard_map/all_gather | solution.py:160
  13.0 345.1 %all-gather.29.cloned.1.call-start = ((), (), s32[]{:S(2)}) async-start(), calls=%async_computation.26 | async-start | bytes 2228224 | tf_op jit(solution)/shard_map/all_gather | solution.py:167
  13.6 351.5 %all-gather.31.cloned.1.call-start = ((), (), s32[]{:S(2)}) async-start(), calls=%async_computation.27 | async-start | bytes 2228224 | tf_op jit(solution)/shard_map/all_gather | solution.py:168
  13.7 205.9 %collective-permute-start = (bf16[128]{0:T(256)(128)(2,1)S(1)}, bf16[128]{0:T(256)(128)(2,1)S(1)}, u32[]{:S(2)}, u32[]{:S(2)}) collective-permute-start(bf16[128]{0:T(256)(128)(2,1)S(1)} %get-tuple-element.163), channel_id=1, source_target_pairs={{0,1},{1,2},{2,3},{3,4},{4,5},{5,6},{6,7},{7,8},{8,9},{9,10},{10,1... | collective-permute-start | bytes 776 | tf_op jit(solution)/shard_map/ppermute | solution.py:28
  14.2 205.8 %collective-permute-start.1 = (bf16[128]{0:T(256)(128)(2,1)S(1)}, bf16[128]{0:T(256)(128)(2,1)S(1)}, u32[]{:S(2)}, u32[]{:S(2)}) collective-permute-start(bf16[128]{0:T(256)(128)(2,1)S(1)} %get-tuple-element.163), channel_id=1, source_target_pairs={{0,15},{1,0},{2,1},{3,2},{4,3},{5,4},{6,5},{7,6},{8,7},{9,8},{10,9... | collective-permute-start | bytes 776 | tf_op jit(solution)/shard_map/ppermute | solution.py:36
  19.2 204.8 %collective-permute-start.15 = (bf16[128]{0:T(256)(128)(2,1)S(1)}, bf16[128]{0:T(256)(128)(2,1)S(1)}, u32[]{:S(2)}, u32[]{:S(2)}) collective-permute-start(bf16[128]{0:T(256)(128)(2,1)S(1)} %get-tuple-element.162), channel_id=1, source_target_pairs={{0,1},{1,2},{2,3},{3,4},{4,5},{5,6},{6,7},{7,8},{8,9},{9,10},{10,1... | collective-permute-start | bytes 776 | tf_op jit(solution)/shard_map/ppermute | solution.py:28
  19.2 205.2 %collective-permute-start.16 = (bf16[128]{0:T(256)(128)(2,1)S(1)}, bf16[128]{0:T(256)(128)(2,1)S(1)}, u32[]{:S(2)}, u32[]{:S(2)}) collective-permute-start(bf16[128]{0:T(256)(128)(2,1)S(1)} %get-tuple-element.162), channel_id=1, source_target_pairs={{0,15},{1,0},{2,1},{3,2},{4,3},{5,4},{6,5},{7,6},{8,7},{9,8},{10,9... | collective-permute-start | bytes 776 | tf_op jit(solution)/shard_map/ppermute | solution.py:36
  23.7 571.1 %reduce-scatter.33.cloned.1.call-start = ((), (), s32[]{:S(2)}) async-start(), calls=%async_computation.17 | async-start | bytes 557056 | tf_op jit(solution)/shard_map/reduce_scatter | solution.py:332
  484.1 165.4 %reduce-scatter.27.cloned.1.call-start = ((), (), s32[]{:S(2)}) async-start(), calls=%async_computation.14 | async-start | bytes 1671168 | tf_op jit(solution)/shard_map/reduce_scatter | solution.py:329
  490.2 221.9 %reduce-scatter.29.cloned.1.call-start = ((), (), s32[]{:S(2)}) async-start(), calls=%async_computation.15 | async-start | bytes 1671168 | tf_op jit(solution)/shard_map/reduce_scatter | solution.py:329
  492.1 284.3 %reduce-scatter.37.cloned.1.call-start = ((), (), s32[]{:S(2)}) async-start(), calls=%async_computation.19 | async-start | bytes 2228224 | tf_op jit(solution)/shard_map/reduce_scatter | solution.py:346
  495.3 345.7 %reduce-scatter.35.cloned.1.call-start = ((), (), s32[]{:S(2)}) async-start(), calls=%async_computation.18 | async-start | bytes 2228224 | tf_op jit(solution)/shard_map/reduce_scatter | solution.py:346
  498.6 406.8 %reduce-scatter.39.cloned.1.call-start = ((), (), s32[]{:S(2)}) async-start(), calls=%async_computation.20 | async-start | bytes 2228224 | tf_op jit(solution)/shard_map/reduce_scatter | solution.py:349
  501.9 468.2 %reduce-scatter.41.cloned.1.call-start = ((), (), s32[]{:S(2)}) async-start(), calls=%async_computation.21 | async-start | bytes 2228224 | tf_op jit(solution)/shard_map/reduce_scatter | solution.py:349
  505.3 522.3 %reduce-scatter.47.cloned.1.call-start = ((), (), s32[]{:S(2)}) async-start(), calls=%async_computation.30 | async-start | bytes 139264
  521.1 563.9 %reduce-scatter.49.cloned.1.call-start = ((), (), s32[]{:S(2)}) async-start(), calls=%async_computation.31 | async-start | bytes 139264
  552.1 590.4 %reduce-scatter.43.cloned.1.call-start = ((), (), s32[]{:S(2)}) async-start(), calls=%async_computation.28 | async-start | bytes 139264
  553.1 647.4 %reduce-scatter.45.cloned.1.call-start = ((), (), s32[]{:S(2)}) async-start(), calls=%async_computation.29 | async-start | bytes 139264
  554.5 703.6 %reduce-scatter.51.cloned.1.call-start = ((), (), s32[]{:S(2)}) async-start(), calls=%async_computation.32 | async-start | bytes 139264
  557.0 758.5 %reduce-scatter.53.cloned.1.call-start = ((), (), s32[]{:S(2)}) async-start(), calls=%async_computation.33 | async-start | bytes 139264
  594.8 757.7 %all-reduce.7.cloned.1.call-start = ((), (), s32[]{:S(2)}) async-start(), calls=%async_computation.34 | async-start | bytes 1572864 | tf_op jit(solution)/shard_map/psum | solution.py:99
  (143 other events, 2573.9 us)
Sparse Core Ops, SparseCore 0:
  10.9 42.5 all-gather.20
  56.3 41.4 all-gather.22
  100.5 41.1 all-gather.24
  143.8 40.6 all-gather.26
  187.1 40.6 all-gather.28
  230.4 40.1 all-gather.30
  474.8 53.0 reduce-scatter.32
  532.5 54.8 reduce-scatter.30
  591.0 58.4 reduce-scatter.26
  653.5 58.4 reduce-scatter.28
  715.8 60.6 reduce-scatter.36
  780.5 60.5 reduce-scatter.34
  844.8 60.5 reduce-scatter.38
  909.5 60.5 reduce-scatter.40
  973.4 54.1 reduce-scatter.46
  1030.9 54.0 reduce-scatter.48
  1088.3 54.0 reduce-scatter.42
  1146.3 54.1 reduce-scatter.44
  1203.9 54.0 reduce-scatter.50
  1261.4 54.0 reduce-scatter.52
  1318.5 33.8 all-reduce.6
